TPU v7x, 32 devices: a whole 2x2x4 slice. The times are simulated.
32 devices in a mesh: prow: 4 (over y, core), pcol: 8 (over z, x).
Axes of the slice: x: 2, y: 2, z: 4, core: 2. Of those that a mesh axis runs over, the one named last changes fastest.
Arguments:
- right_side: float32 [8, 256, 128], P(None, 'prow'), may hold values from -6 to 6
- lower_prev: float32 [8, 256, 129024], P(None, 'prow', 'pcol'), may hold values from -0.015625 to 0.015625
- solved_prev: float32 [129024, 128], P('pcol'), may hold values from -6 to 6
- lower_window: float32 [8, 256, 2048], P(None, 'prow', 'pcol'), may hold values from -0.1875 to 0.1875
- inverse_diag: float32 [8, 256, 256], P(None, 'prow'), may hold values from -0.25 to 1.4, as said below
Outputs:
- solution: float32 [8, 256, 128], P(None, 'prow')
Inputs may be any that keep to these rules, and one draw needn't show every extreme that they name: `inverse_diag`: each block is lower triangular: zero above its diagonal, with diagonal entries of 0.7 to 1.4.
All inputs are finite; a program needn't handle non-finite values.
Results may differ from a plain program's by a relative error of at most 0.00011.
Values sent between devices are 32-bit elements; how exact they have to be, the bound alone decides.
No kernel may reach another device: no remote copies, remote signals or barrier semaphores. Data moves between devices by JAX's collectives and lax.ppermute only.
A program may use at most 128 MiB of HBM per device.

v0:
```python
import jax
import jax.numpy as jnp
from jax import lax
from jax.sharding import PartitionSpec as P


def local(right_side, lower_prev, solved_prev, lower_window, inverse_diag):
    highest = lax.Precision.HIGHEST
    blocks = right_side.shape[0]
    local_rows = right_side.shape[1]
    columns = right_side.shape[2]
    block_rows = inverse_diag.shape[2]
    row_start = lax.axis_index("prow") * local_rows
    solved = jnp.zeros((blocks * block_rows, columns), jnp.float32)
    pieces = []
    full_inverse = lax.all_gather(inverse_diag, "prow", axis=1, tiled=True)
    full_window = lax.all_gather(lower_window, "pcol", axis=2, tiled=True)
    for row_block in range(blocks):
        window_term = jnp.dot(
            full_window[row_block], solved, precision=highest, preferred_element_type=jnp.float32
        )
        earlier_part = jnp.dot(
            lower_prev[row_block],
            solved_prev,
            precision=highest,
            preferred_element_type=jnp.float32,
        )
        earlier_here = lax.psum(earlier_part, "pcol")
        local_residual = right_side[row_block] - (earlier_here + window_term)
        residual = lax.all_gather(local_residual, "prow", axis=0, tiled=True)
        whole_rows = jnp.dot(
            full_inverse[row_block], residual, precision=highest, preferred_element_type=jnp.float32
        )
        pieces.append(lax.dynamic_slice_in_dim(whole_rows, row_start, local_rows, 0))
        solved = lax.dynamic_update_slice_in_dim(solved, whole_rows, row_block * block_rows, 0)
    return jnp.stack(pieces)


def solution(mesh):
    in_specs = (
        P(None, "prow", None),
        P(None, "prow", "pcol"),
        P("pcol", None),
        P(None, "prow", "pcol"),
        P(None, "prow", None),
    )
    out_specs = P(None, "prow", None)
    return jax.shard_map(local, mesh=mesh, in_specs=in_specs, out_specs=out_specs, check_vma=False)
```

profile of v0, /device:TPU:0, one launch (start us, length us, event | category | flops | bytes accessed | tf_op | source)
XLA Modules:
  0.0 249.5 jit_solution(15784132453054589347)
XLA Ops:
  6.5 0.7 all-gather.3.cloned.1.call-update
  7.3 10.3 %fusion.4 = f32[64,128]{1,0:T(8,128)} fusion(f32[16128,128]{1,0:T(8,128)} %param.7, f32[8,64,16128]{2,1,0:T(8,128)} %param.6), kind=kOutput, calls=%fused_computation.4 | convolution fusion | flops 1585446912 | bytes 12419072 | tf_op jit(solution)/shard_map/dot_general | solution.py:22
  17.7 8.1 %fusion.6 = f32[64,128]{1,0:T(8,128)} fusion(f32[16128,128]{1,0:T(8,128)S(1)} %copy-done, f32[8,64,16128]{2,1,0:T(8,128)} %param.6), kind=kOutput, calls=%fused_computation.6 | convolution fusion | flops 1585446912 | bytes 12419072 | tf_op jit(solution)/shard_map/dot_general | solution.py:22
  25.8 7.9 %fusion.8 = f32[64,128]{1,0:T(8,128)} fusion(f32[16128,128]{1,0:T(8,128)S(1)} %copy-done, f32[8,64,16128]{2,1,0:T(8,128)} %param.6), kind=kOutput, calls=%fused_computation.8 | convolution fusion | flops 1585446912 | bytes 12419072 | tf_op jit(solution)/shard_map/dot_general | solution.py:22
  33.7 8.1 %fusion.10 = f32[64,128]{1,0:T(8,128)} fusion(f32[16128,128]{1,0:T(8,128)S(1)} %copy-done, f32[8,64,16128]{2,1,0:T(8,128)} %param.6), kind=kOutput, calls=%fused_computation.10 | convolution fusion | flops 1585446912 | bytes 12419072 | tf_op jit(solution)/shard_map/dot_general | solution.py:22
  41.8 7.9 %fusion.12 = f32[64,128]{1,0:T(8,128)} fusion(f32[16128,128]{1,0:T(8,128)S(1)} %copy-done, f32[8,64,16128]{2,1,0:T(8,128)} %param.6), kind=kOutput, calls=%fused_computation.12 | convolution fusion | flops 1585446912 | bytes 12419072 | tf_op jit(solution)/shard_map/dot_general | solution.py:22
  49.7 8.4 %fusion.14 = f32[64,128]{1,0:T(8,128)} fusion(f32[16128,128]{1,0:T(8,128)S(1)} %copy-done, f32[8,64,16128]{2,1,0:T(8,128)} %param.6), kind=kOutput, calls=%fused_computation.14 | convolution fusion | flops 1585446912 | bytes 12419072 | tf_op jit(solution)/shard_map/dot_general | solution.py:22
  58.1 7.9 %fusion = f32[64,128]{1,0:T(8,128)} fusion(f32[16128,128]{1,0:T(8,128)S(1)} %copy-done, f32[8,64,16128]{2,1,0:T(8,128)} %param.6), kind=kOutput, calls=%fused_computation | convolution fusion | flops 1585446912 | bytes 12419072 | tf_op jit(solution)/shard_map/dot_general | solution.py:22
  66.1 8.2 %fusion.2 = f32[64,128]{1,0:T(8,128)} fusion(f32[16128,128]{1,0:T(8,128)S(1)} %copy-done, f32[8,64,16128]{2,1,0:T(8,128)} %param.6), kind=kOutput, calls=%fused_computation.2 | convolution fusion | flops 1585446912 | bytes 12419072 | tf_op jit(solution)/shard_map/dot_general | solution.py:22
  74.3 0.7 all-gather.5.cloned.1.call-update
  75.0 12.2 %all-gather.3.cloned.1.call-done = f32[8,64,2048]{2,1,0:T(8,128)} async-done(((f32[8,64,256]{2,1,0:T(8,128)}), f32[8,64,2048]{2,1,0:T(8,128)}) %all-gather.3.cloned.1.call-update) | async-done | bytes 4194320 | tf_op jit(solution)/shard_map/all_gather | solution.py:17
  87.1 1.2 fusion.38
  88.3 73.8 %all-reduce.4.cloned.1.call-done = (f32[64,128]{1,0:T(8,128)}, f32[64,128]{1,0:T(8,128)}, f32[64,128]{1,0:T(8,128)}, f32[64,128]{1,0:T(8,128)}, f32[64,128]{1,0:...) async-done(((f32[64,128]{1,0:T(8,128)}, f32[64,128]{1,0:T(8,128)}, f32[64,128]{1,0:T(8,128)}, f32[64,128]{1,0:T(8,128)}, f32[64,128]{1,0:T(8,128)}, ...) | async-done | bytes 262160 | tf_op jit(solution)/shard_map/psum | solution.py:28
  162.1 0.8 bitcast_subtract_fusion
  163.0 5.4 %all_gather.31 = f32[256,128]{1,0:T(8,128)S(1)} all-gather(f32[64,128]{1,0:T(8,128)S(1)} %bitcast_subtract_fusion), channel_id=1, replica_groups=mesh['prow'=4,'pcol'=8] {'prow'}, dimensions={0}, use_global_device_ids=true | all-gather | bytes 163840 | tf_op jit(solution)/shard_map/all_gather | solution.py:30
  168.4 17.4 %all-gather.5.cloned.1.call-done = f32[8,256,256]{2,1,0:T(8,128)} async-done(((f32[8,64,256]{2,1,0:T(8,128)}), f32[8,256,256]{2,1,0:T(8,128)}) %all-gather.5.cloned.1.call-update) | async-done | bytes 2097168 | tf_op jit(solution)/shard_map/all_gather | solution.py:16
  185.8 1.5 fusion.47
  187.3 2.1 fusion.25
  189.4 5.4 %all_gather.33 = f32[256,128]{1,0:T(8,128)S(1)} all-gather(f32[64,128]{1,0:T(8,128)S(1)} %fusion.25), channel_id=1, replica_groups=mesh['prow'=4,'pcol'=8] {'prow'}, dimensions={0}, use_global_device_ids=true | all-gather | bytes 163840 | tf_op jit(solution)/shard_map/all_gather | solution.py:30
  194.8 0.1 bitcast_dynamic-update-slice_fusion.13
  194.9 0.1 dynamic_update_slice.21
  195.0 1.4 bitcast_dynamic-update-slice_fusion.5
  196.4 2.3 fusion.27
  198.7 5.4 %all_gather.34 = f32[256,128]{1,0:T(8,128)S(1)} all-gather(f32[64,128]{1,0:T(8,128)S(1)} %fusion.27), channel_id=1, replica_groups=mesh['prow'=4,'pcol'=8] {'prow'}, dimensions={0}, use_global_device_ids=true | all-gather | bytes 163840 | tf_op jit(solution)/shard_map/all_gather | solution.py:30
  204.1 1.4 bitcast_dynamic-update-slice_fusion.4
  205.5 1.2 fusion.29
  206.7 5.6 %all_gather.35 = f32[256,128]{1,0:T(8,128)S(1)} all-gather(f32[64,128]{1,0:T(8,128)S(1)} %fusion.29), channel_id=1, replica_groups=mesh['prow'=4,'pcol'=8] {'prow'}, dimensions={0}, use_global_device_ids=true | all-gather | bytes 163840 | tf_op jit(solution)/shard_map/all_gather | solution.py:30
  212.3 0.4 bitcast_dynamic-update-slice_fusion.3
  212.7 1.2 fusion.31
  213.9 5.4 %all_gather.36 = f32[256,128]{1,0:T(8,128)S(1)} all-gather(f32[64,128]{1,0:T(8,128)S(1)} %fusion.31), channel_id=1, replica_groups=mesh['prow'=4,'pcol'=8] {'prow'}, dimensions={0}, use_global_device_ids=true | all-gather | bytes 163840 | tf_op jit(solution)/shard_map/all_gather | solution.py:30
  219.4 0.4 bitcast_dynamic-update-slice_fusion.2
  219.8 1.2 fusion.33
  221.0 5.4 %all_gather.37 = f32[256,128]{1,0:T(8,128)S(1)} all-gather(f32[64,128]{1,0:T(8,128)S(1)} %fusion.33), channel_id=1, replica_groups=mesh['prow'=4,'pcol'=8] {'prow'}, dimensions={0}, use_global_device_ids=true | all-gather | bytes 163840 | tf_op jit(solution)/shard_map/all_gather | solution.py:30
  226.4 0.4 bitcast_dynamic-update-slice_fusion.1
  226.9 1.2 fusion.35
  228.1 5.6 %all_gather.38 = f32[256,128]{1,0:T(8,128)S(1)} all-gather(f32[64,128]{1,0:T(8,128)S(1)} %fusion.35), channel_id=1, replica_groups=mesh['prow'=4,'pcol'=8] {'prow'}, dimensions={0}, use_global_device_ids=true | all-gather | bytes 163840 | tf_op jit(solution)/shard_map/all_gather | solution.py:30
  233.7 0.4 bitcast_dynamic-update-slice_fusion
  234.2 1.2 fusion.37
  235.4 5.4 %all_gather.39 = f32[256,128]{1,0:T(8,128)S(1)} all-gather(f32[64,128]{1,0:T(8,128)S(1)} %fusion.37), channel_id=1, replica_groups=mesh['prow'=4,'pcol'=8] {'prow'}, dimensions={0}, use_global_device_ids=true | all-gather | bytes 163840 | tf_op jit(solution)/shard_map/all_gather | solution.py:30
  240.8 0.1 bitcast_dynamic-update-slice_fusion.12
  240.9 0.1 bitcast_dynamic-update-slice_fusion.11
  241.0 0.1 bitcast_dynamic-update-slice_fusion.10
  241.1 0.1 bitcast_dynamic-update-slice_fusion.9
  241.2 0.1 bitcast_dynamic-update-slice_fusion.8
  241.2 0.1 bitcast_dynamic-update-slice_fusion.7
  241.3 0.4 fusion.40
  241.7 0.1 bitcast_dynamic-update-slice_fusion.6
  241.8 0.9 copy.7
  (22 shorter events, 0.1 us)
Async XLA Ops:
  6.5 80.6 %all-gather.3.cloned.1.call-start = ((), (), s32[]{:S(2)}) async-start(), calls=%async_computation | async-start | bytes 4718592 | tf_op jit(solution)/shard_map/all_gather | solution.py:17
  7.3 154.9 %all-reduce.4.cloned.1.call-start = ((), (), s32[]{:S(2)}) async-start(), calls=%async_computation.2 | async-start | bytes 524288 | tf_op jit(solution)/shard_map/psum | solution.py:28
  7.3 10.4 %copy-start = (f32[16128,128]{1,0:T(8,128)S(1)}, f32[16128,128]{1,0:T(8,128)}, u32[]{:S(2)}) copy-start(f32[16128,128]{1,0:T(8,128)} %param.7) | copy-start | bytes 24772612
  66.1 96.1 %copy-start.3 = (f32[8,64,128]{2,1,0:T(8,128)S(1)}, f32[8,64,128]{2,1,0:T(8,128)}, u32[]{:S(2)}) copy-start(f32[8,64,128]{2,1,0:T(8,128)} %param.5) | copy-start | bytes 786436
  74.2 111.6 %all-gather.5.cloned.1.call-start = ((), (), s32[]{:S(2)}) async-start(), calls=%async_computation.1 | async-start | bytes 2621440 | tf_op jit(solution)/shard_map/all_gather | solution.py:16
  162.1 43.4 %copy-start.8 = (f32[64,128]{1,0:T(8,128)S(1)}, f32[64,128]{1,0:T(8,128)}, u32[]{:S(2)}) copy-start(f32[64,128]{1,0:T(8,128)} %get-tuple-element.8) | copy-start | bytes 98308
  168.4 44.3 %copy-start.7 = (f32[64,128]{1,0:T(8,128)S(1)}, f32[64,128]{1,0:T(8,128)}, u32[]{:S(2)}) copy-start(f32[64,128]{1,0:T(8,128)} %get-tuple-element.9) | copy-start | bytes 98308
  185.8 19.7 %copy-start.1 = (f32[8,64,2048]{2,1,0:T(8,128)S(1)}, f32[8,64,2048]{2,1,0:T(8,128)}, u32[]{:S(2)}) copy-start(f32[8,64,2048]{2,1,0:T(8,128)} %all-gather.3.cloned.1.call-done) | copy-start | bytes 12582916
  185.8 26.5 %copy-start.2 = (f32[8,256,256]{2,1,0:T(8,128)S(1)}, f32[8,256,256]{2,1,0:T(8,128)}, u32[]{:S(2)}) copy-start(f32[8,256,256]{2,1,0:T(8,128)} %all-gather.5.cloned.1.call-done) | copy-start | bytes 6291460
  195.0 24.8 %copy-start.6 = (f32[64,128]{1,0:T(8,128)S(1)}, f32[64,128]{1,0:T(8,128)}, u32[]{:S(2)}) copy-start(f32[64,128]{1,0:T(8,128)} %get-tuple-element.10) | copy-start | bytes 98308
  198.7 28.2 %copy-start.5 = (f32[64,128]{1,0:T(8,128)S(1)}, f32[64,128]{1,0:T(8,128)}, u32[]{:S(2)}) copy-start(f32[64,128]{1,0:T(8,128)} %get-tuple-element.11) | copy-start | bytes 98308
  206.7 27.4 %copy-start.4 = (f32[64,128]{1,0:T(8,128)S(1)}, f32[64,128]{1,0:T(8,128)}, u32[]{:S(2)}) copy-start(f32[64,128]{1,0:T(8,128)} %get-tuple-element.12) | copy-start | bytes 98308
Sparse Core Ops, SparseCore 0:
  9.4 77.7 all-gather.2
  91.4 70.6 all-reduce.3
  163.8 21.9 all-gather.4
where the time goes:
time: 253 us; the launch traced here: 249 us
  waiting for transfers between devices  105 us (42%)
  matrix products  83.6 us (33%)
  blocking collectives  43.7 us (17%)
  between operations  13.6 us (5%)
    psum x1, waiting for transfers between devices, local(): earlier_here = lax.psum(earlier_part, 'pcol')  73.8 us
    dot_general x8, matrix products, local(): jnp.dot(lower_prev[row_block], solved_prev, precision=highest, preferred_...  66.9 us
    all_gather x8, blocking collectives, local(): residual = lax.all_gather(local_residual, 'prow', axis=0, tiled=True)  43.7 us
    all_gather x1, waiting for transfers between devices, local(): full_inverse = lax.all_gather(inverse_diag, 'prow', axis=1, tiled=True)  17.4 us
    all_gather x1, waiting for transfers between devices, local(): full_window = lax.all_gather(lower_window, 'pcol', axis=2, tiled=True)  12.2 us
    dot_general x7, matrix products, local(): jnp.dot(full_window[row_block], solved, precision=highest, preferred_elem...  10.4 us
    dot_general x8, matrix products, local(): jnp.dot(full_inverse[row_block], residual, precision=highest, preferred_e...  6.33 us
  transfers between devices with their start and end apart: 3, of which 3 were waited for; matrix products, arithmetic and copies ran while one was open for 28% of the time, Pallas kernels for 0%

commit v1 on v0

--- a/solution.py
+++ b/solution.py
@@ -27,7 +27,18 @@
         )
         earlier_here = lax.psum(earlier_part, "pcol")
         local_residual = right_side[row_block] - (earlier_here + window_term)
-        residual = lax.all_gather(local_residual, "prow", axis=0, tiled=True)
+        ways = lax.axis_size("prow")
+        up = [(d, (d + 1) % ways) for d in range(ways)]
+        down = [(d, (d - 1) % ways) for d in range(ways)]
+        earlier, later = ([local_residual], [local_residual])
+        for _ in range(ways // 2):
+            earlier.append(lax.ppermute(earlier[-1], "prow", up))
+        for _ in range((ways - 1) // 2):
+            later.append(lax.ppermute(later[-1], "prow", down))
+        line = jnp.concatenate([*earlier[::-1], *later[1:]], axis=0)
+        residual = jnp.roll(
+            line, (lax.axis_index("prow") - ways // 2) * local_residual.shape[0], axis=0
+        )
         whole_rows = jnp.dot(
             full_inverse[row_block], residual, precision=highest, preferred_element_type=jnp.float32
         )

time: 253 us -> 273 us (1.079)
  blocking collectives: 43.7 us -> 0 us
  waiting for transfers between devices: 105 us -> 142 us
  starting transfers between devices: 0.08 us -> 14.7 us
  matrix products: 83.6 us -> 95.3 us
    all_gather x8 -> x0, blocking collectives: 43.7 us -> none  [local(): residual = lax.all_gather(local_residual, 'prow', axis=0, tiled=True)]
    ppermute x0 -> x24, waiting for transfers between devices: none -> 35.2 us  [the longest x16 35.1 us: local(): earlier.append(lax.ppermute(earlier[-1], 'prow', up))]
    ppermute x0 -> x24, starting transfers between devices: none -> 14.6 us  [the longest x8 13.8 us: local(): later.append(lax.ppermute(later[-1], 'prow', down))]
    dot_general x8, matrix products: 6.33 us -> 13.2 us  [local(): jnp.dot(full_inverse[row_block], residual, precision=highest, preferred_e...]
    dot_general x7, matrix products: 10.4 us -> 15.2 us  [local(): jnp.dot(full_window[row_block], solved, precision=highest, preferred_elem...]
  transfers between devices with their start and end apart: 3 -> 27, of which waited for: 3 -> 20; matrix products, arithmetic and copies ran while one was open for 28% -> 26% of each run, Pallas kernels for 0% -> 0%
where the time goes in v1:
time: 273 us; the launch traced here: 269 us
  waiting for transfers between devices  142 us (52%)
  matrix products  95.3 us (35%)
  starting transfers between devices  14.7 us (5%)
  between operations  13.7 us (5%)
    psum x1, waiting for transfers between devices, local(): earlier_here = lax.psum(earlier_part, 'pcol')  73.8 us
    dot_general x8, matrix products, local(): jnp.dot(lower_prev[row_block], solved_prev, precision=highest, preferred_...  66.9 us
    ppermute x16, waiting for transfers between devices, local(): earlier.append(lax.ppermute(earlier[-1], 'prow', up))  35.1 us
    all_gather x1, waiting for transfers between devices, local(): full_inverse = lax.all_gather(inverse_diag, 'prow', axis=1, tiled=True)  19.5 us
    dot_general x7, matrix products, local(): jnp.dot(full_window[row_block], solved, precision=highest, preferred_elem...  15.2 us
    ppermute x8, starting transfers between devices, local(): later.append(lax.ppermute(later[-1], 'prow', down))  13.8 us
    dot_general x8, matrix products, local(): jnp.dot(full_inverse[row_block], residual, precision=highest, preferred_e...  13.2 us
    all_gather x1, waiting for transfers between devices, local(): full_window = lax.all_gather(lower_window, 'pcol', axis=2, tiled=True)  12.1 us
  transfers between devices with their start and end apart: 27, of which 20 were waited for; matrix products, arithmetic and copies ran while one was open for 26% of the time, Pallas kernels for 0%

profile of v1, /device:TPU:0, one launch (start us, length us, event | category | flops | bytes accessed | tf_op | source)
XLA Modules:
  0.0 269.3 jit_solution(6868114484970018094)
XLA Ops:
  7.3 10.4 %fusion.4 = f32[64,128]{1,0:T(8,128)} fusion(f32[16128,128]{1,0:T(8,128)} %param.9, f32[8,64,16128]{2,1,0:T(8,128)} %param.8), kind=kOutput, calls=%fused_computation.4 | convolution fusion | flops 1585446912 | bytes 12419072 | tf_op jit(solution)/shard_map/dot_general | solution.py:22
  17.7 8.1 %fusion.6 = f32[64,128]{1,0:T(8,128)} fusion(f32[16128,128]{1,0:T(8,128)S(1)} %copy-done, f32[8,64,16128]{2,1,0:T(8,128)} %param.8), kind=kOutput, calls=%fused_computation.6 | convolution fusion | flops 1585446912 | bytes 12419072 | tf_op jit(solution)/shard_map/dot_general | solution.py:22
  25.8 7.9 %fusion.8 = f32[64,128]{1,0:T(8,128)} fusion(f32[16128,128]{1,0:T(8,128)S(1)} %copy-done, f32[8,64,16128]{2,1,0:T(8,128)} %param.8), kind=kOutput, calls=%fused_computation.8 | convolution fusion | flops 1585446912 | bytes 12419072 | tf_op jit(solution)/shard_map/dot_general | solution.py:22
  33.7 8.1 %fusion.10 = f32[64,128]{1,0:T(8,128)} fusion(f32[16128,128]{1,0:T(8,128)S(1)} %copy-done, f32[8,64,16128]{2,1,0:T(8,128)} %param.8), kind=kOutput, calls=%fused_computation.10 | convolution fusion | flops 1585446912 | bytes 12419072 | tf_op jit(solution)/shard_map/dot_general | solution.py:22
  41.8 7.9 %fusion.12 = f32[64,128]{1,0:T(8,128)} fusion(f32[16128,128]{1,0:T(8,128)S(1)} %copy-done, f32[8,64,16128]{2,1,0:T(8,128)} %param.8), kind=kOutput, calls=%fused_computation.12 | convolution fusion | flops 1585446912 | bytes 12419072 | tf_op jit(solution)/shard_map/dot_general | solution.py:22
  49.7 8.4 %fusion.14 = f32[64,128]{1,0:T(8,128)} fusion(f32[16128,128]{1,0:T(8,128)S(1)} %copy-done, f32[8,64,16128]{2,1,0:T(8,128)} %param.8), kind=kOutput, calls=%fused_computation.14 | convolution fusion | flops 1585446912 | bytes 12419072 | tf_op jit(solution)/shard_map/dot_general | solution.py:22
  58.1 7.9 %fusion = f32[64,128]{1,0:T(8,128)} fusion(f32[16128,128]{1,0:T(8,128)S(1)} %copy-done, f32[8,64,16128]{2,1,0:T(8,128)} %param.8), kind=kOutput, calls=%fused_computation | convolution fusion | flops 1585446912 | bytes 12419072 | tf_op jit(solution)/shard_map/dot_general | solution.py:22
  66.1 8.1 %fusion.2 = f32[64,128]{1,0:T(8,128)} fusion(f32[16128,128]{1,0:T(8,128)S(1)} %copy-done, f32[8,64,16128]{2,1,0:T(8,128)} %param.8), kind=kOutput, calls=%fused_computation.2 | convolution fusion | flops 1585446912 | bytes 12419072 | tf_op jit(solution)/shard_map/dot_general | solution.py:22
  75.0 12.1 %all-gather.3.cloned.1.call-done = f32[8,64,2048]{2,1,0:T(8,128)} async-done(((f32[8,64,256]{2,1,0:T(8,128)}), f32[8,64,2048]{2,1,0:T(8,128)}) %all-gather.3.cloned.1.call-update) | async-done | bytes 4194320 | tf_op jit(solution)/shard_map/all_gather | solution.py:17
  88.3 73.8 %all-reduce.4.cloned.1.call-done = (f32[64,128]{1,0:T(8,128)}, f32[64,128]{1,0:T(8,128)}, f32[64,128]{1,0:T(8,128)}, f32[64,128]{1,0:T(8,128)}, f32[64,128]{1,0:...) async-done(((f32[64,128]{1,0:T(8,128)}, f32[64,128]{1,0:T(8,128)}, f32[64,128]{1,0:T(8,128)}, f32[64,128]{1,0:T(8,128)}, f32[64,128]{1,0:T(8,128)}, ...) | async-done | bytes 262160 | tf_op jit(solution)/shard_map/psum | solution.py:28
  163.0 1.7 collective-permute-start.2
  164.7 1.6 collective-permute-done
  166.3 19.5 %all-gather.5.cloned.1.call-done = f32[8,256,256]{2,1,0:T(8,128)} async-done(((f32[8,64,256]{2,1,0:T(8,128)}), f32[8,256,256]{2,1,0:T(8,128)}) %all-gather.5.cloned.1.call-update) | async-done | bytes 2097168 | tf_op jit(solution)/shard_map/all_gather | solution.py:16
  185.8 1.6 fusion.47
  187.4 1.7 fusion.25
  189.4 1.5 collective-permute-start.5
  190.9 1.6 collective-permute-done.3
  192.6 3.2 %collective-permute-done.4 = f32[64,128]{1,0:T(8,128)S(1)} collective-permute-done((f32[64,128]{1,0:T(8,128)S(1)}, f32[64,128]{1,0:T(8,128)S(1)}, u32[]{:S(2)}, u32[]{:S(2)}) %collective-permute-start.4) | collective-permute-done | bytes 32800 | tf_op jit(solution)/shard_map/ppermute | solution.py:35
  195.8 1.7 bitcast_dynamic-update-slice_fusion.5
  197.5 2.3 fusion.27
  199.8 1.7 collective-permute-start.8
  201.6 1.6 collective-permute-done.6
  203.2 3.3 %collective-permute-done.7 = f32[64,128]{1,0:T(8,128)S(1)} collective-permute-done((f32[64,128]{1,0:T(8,128)S(1)}, f32[64,128]{1,0:T(8,128)S(1)}, u32[]{:S(2)}, u32[]{:S(2)}) %collective-permute-start.7) | collective-permute-done | bytes 32800 | tf_op jit(solution)/shard_map/ppermute | solution.py:35
  206.5 1.7 bitcast_dynamic-update-slice_fusion.4
  208.2 2.2 fusion.29
  210.5 1.7 collective-permute-start.11
  212.2 1.6 collective-permute-done.9
  213.8 3.3 %collective-permute-done.10 = f32[64,128]{1,0:T(8,128)S(1)} collective-permute-done((f32[64,128]{1,0:T(8,128)S(1)}, f32[64,128]{1,0:T(8,128)S(1)}, u32[]{:S(2)}, u32[]{:S(2)}) %collective-permute-start.10) | collective-permute-done | bytes 32800 | tf_op jit(solution)/shard_map/ppermute | solution.py:35
  217.2 1.7 bitcast_dynamic-update-slice_fusion.3
  218.8 2.2 fusion.31
  221.2 1.7 collective-permute-start.14
  222.9 1.6 collective-permute-done.12
  224.6 3.2 %collective-permute-done.13 = f32[64,128]{1,0:T(8,128)S(1)} collective-permute-done((f32[64,128]{1,0:T(8,128)S(1)}, f32[64,128]{1,0:T(8,128)S(1)}, u32[]{:S(2)}, u32[]{:S(2)}) %collective-permute-start.13) | collective-permute-done | bytes 32800 | tf_op jit(solution)/shard_map/ppermute | solution.py:35
  227.8 1.7 bitcast_dynamic-update-slice_fusion.2
  229.5 2.2 fusion.33
  231.9 1.8 collective-permute-start.17
  233.7 1.5 collective-permute-done.15
  235.4 3.2 %collective-permute-done.16 = f32[64,128]{1,0:T(8,128)S(1)} collective-permute-done((f32[64,128]{1,0:T(8,128)S(1)}, f32[64,128]{1,0:T(8,128)S(1)}, u32[]{:S(2)}, u32[]{:S(2)}) %collective-permute-start.16) | collective-permute-done | bytes 32800 | tf_op jit(solution)/shard_map/ppermute | solution.py:35
  238.7 1.7 bitcast_dynamic-update-slice_fusion.1
  240.3 2.2 fusion.35
  242.7 1.8 collective-permute-start.20
  244.5 1.5 collective-permute-done.18
  246.1 3.2 %collective-permute-done.19 = f32[64,128]{1,0:T(8,128)S(1)} collective-permute-done((f32[64,128]{1,0:T(8,128)S(1)}, f32[64,128]{1,0:T(8,128)S(1)}, u32[]{:S(2)}, u32[]{:S(2)}) %collective-permute-start.19) | collective-permute-done | bytes 32800 | tf_op jit(solution)/shard_map/ppermute | solution.py:35
  249.3 1.7 bitcast_dynamic-update-slice_fusion
  251.0 2.2 fusion.37
  253.4 1.8 collective-permute-start.23
  256.8 3.2 %collective-permute-done.22 = f32[64,128]{1,0:T(8,128)S(1)} collective-permute-done((f32[64,128]{1,0:T(8,128)S(1)}, f32[64,128]{1,0:T(8,128)S(1)}, u32[]{:S(2)}, u32[]{:S(2)}) %collective-permute-start.22) | collective-permute-done | bytes 32800 | tf_op jit(solution)/shard_map/ppermute | solution.py:35
  260.0 1.6 fusion.40
  (58 shorter events, 7.6 us)
Async XLA Ops:
  6.5 80.6 %all-gather.3.cloned.1.call-start = ((), (), s32[]{:S(2)}) async-start(), calls=%async_computation | async-start | bytes 4718592 | tf_op jit(solution)/shard_map/all_gather | solution.py:17
  7.3 154.9 %all-reduce.4.cloned.1.call-start = ((), (), s32[]{:S(2)}) async-start(), calls=%async_computation.2 | async-start | bytes 524288 | tf_op jit(solution)/shard_map/psum | solution.py:28
  7.3 10.4 %copy-start = (f32[16128,128]{1,0:T(8,128)S(1)}, f32[16128,128]{1,0:T(8,128)}, u32[]{:S(2)}) copy-start(f32[16128,128]{1,0:T(8,128)} %param.9) | copy-start | bytes 24772612
  66.1 96.0 %copy-start.1 = (f32[8,64,128]{2,1,0:T(8,128)S(1)}, f32[8,64,128]{2,1,0:T(8,128)}, u32[]{:S(2)}) copy-start(f32[8,64,128]{2,1,0:T(8,128)} %param.7) | copy-start | bytes 786436
  74.3 111.5 %all-gather.5.cloned.1.call-start = ((), (), s32[]{:S(2)}) async-start(), calls=%async_computation.1 | async-start | bytes 2621440 | tf_op jit(solution)/shard_map/all_gather | solution.py:16
  162.1 46.1 %copy-start.6 = (f32[64,128]{1,0:T(8,128)S(1)}, f32[64,128]{1,0:T(8,128)}, u32[]{:S(2)}) copy-start(f32[64,128]{1,0:T(8,128)} %get-tuple-element.9) | copy-start | bytes 98308
  163.0 3.3 %collective-permute-start = (f32[64,128]{1,0:T(8,128)S(1)}, f32[64,128]{1,0:T(8,128)S(1)}, u32[]{:S(2)}, u32[]{:S(2)}) collective-permute-start(f32[64,128]{1,0:T(8,128)S(1)} %bitcast_subtract_fusion), channel_id=1, source_target_pairs={{0,8},{8,16},{16,24},{24,0},{1,9},{9,17},{17,25},{25,1},{2,10},{10... | collective-permute-start | bytes 98312 | tf_op jit(solution)/shard_map/ppermute | solution.py:35
  163.0 22.8 %collective-permute-start.2 = (f32[64,128]{1,0:T(8,128)S(1)}, f32[64,128]{1,0:T(8,128)S(1)}, u32[]{:S(2)}, u32[]{:S(2)}) collective-permute-start(f32[64,128]{1,0:T(8,128)S(1)} %bitcast_subtract_fusion), channel_id=1, source_target_pairs={{0,24},{8,0},{16,8},{24,16},{1,25},{9,1},{17,9},{25,17},{2,26},{10... | collective-permute-start | bytes 98312 | tf_op jit(solution)/shard_map/ppermute | solution.py:37
  166.3 19.5 %collective-permute-start.1 = (f32[64,128]{1,0:T(8,128)S(1)}, f32[64,128]{1,0:T(8,128)S(1)}, u32[]{:S(2)}, u32[]{:S(2)}) collective-permute-start(f32[64,128]{1,0:T(8,128)S(1)} %collective-permute-done), channel_id=1, source_target_pairs={{0,8},{8,16},{16,24},{24,0},{1,9},{9,17},{17,25},{25,1},{2,10},{10... | collective-permute-start | bytes 98312 | tf_op jit(solution)/shard_map/ppermute | solution.py:35
  166.3 52.5 %copy-start.5 = (f32[64,128]{1,0:T(8,128)S(1)}, f32[64,128]{1,0:T(8,128)}, u32[]{:S(2)}) copy-start(f32[64,128]{1,0:T(8,128)} %get-tuple-element.10) | copy-start | bytes 98308
  189.1 3.4 %collective-permute-start.3 = (f32[64,128]{1,0:T(8,128)S(1)}, f32[64,128]{1,0:T(8,128)S(1)}, u32[]{:S(2)}, u32[]{:S(2)}) collective-permute-start(f32[64,128]{1,0:T(8,128)S(1)} %fusion.25), channel_id=1, source_target_pairs={{0,8},{8,16},{16,24},{24,0},{1,9},{9,17},{17,25},{25,1},{2,10},{10... | collective-permute-start | bytes 98312 | tf_op jit(solution)/shard_map/ppermute | solution.py:35
  189.4 3.2 %collective-permute-start.5 = (f32[64,128]{1,0:T(8,128)S(1)}, f32[64,128]{1,0:T(8,128)S(1)}, u32[]{:S(2)}, u32[]{:S(2)}) collective-permute-start(f32[64,128]{1,0:T(8,128)S(1)} %fusion.25), channel_id=1, source_target_pairs={{0,24},{8,0},{16,8},{24,16},{1,25},{9,1},{17,9},{25,17},{2,26},{10... | collective-permute-start | bytes 98312 | tf_op jit(solution)/shard_map/ppermute | solution.py:37
  192.5 3.3 %collective-permute-start.4 = (f32[64,128]{1,0:T(8,128)S(1)}, f32[64,128]{1,0:T(8,128)S(1)}, u32[]{:S(2)}, u32[]{:S(2)}) collective-permute-start(f32[64,128]{1,0:T(8,128)S(1)} %collective-permute-done.3), channel_id=1, source_target_pairs={{0,8},{8,16},{16,24},{24,0},{1,9},{9,17},{17,25},{25,1},{2,10},{10... | collective-permute-start | bytes 98312 | tf_op jit(solution)/shard_map/ppermute | solution.py:35
  192.6 36.9 %copy-start.4 = (f32[64,128]{1,0:T(8,128)S(1)}, f32[64,128]{1,0:T(8,128)}, u32[]{:S(2)}) copy-start(f32[64,128]{1,0:T(8,128)} %get-tuple-element.11) | copy-start | bytes 98308
  199.8 40.6 %copy-start.3 = (f32[64,128]{1,0:T(8,128)S(1)}, f32[64,128]{1,0:T(8,128)}, u32[]{:S(2)}) copy-start(f32[64,128]{1,0:T(8,128)} %get-tuple-element.12) | copy-start | bytes 98308
  199.8 3.4 %collective-permute-start.6 = (f32[64,128]{1,0:T(8,128)S(1)}, f32[64,128]{1,0:T(8,128)S(1)}, u32[]{:S(2)}, u32[]{:S(2)}) collective-permute-start(f32[64,128]{1,0:T(8,128)S(1)} %fusion.27), channel_id=1, source_target_pairs={{0,8},{8,16},{16,24},{24,0},{1,9},{9,17},{17,25},{25,1},{2,10},{10... | collective-permute-start | bytes 98312 | tf_op jit(solution)/shard_map/ppermute | solution.py:35
  199.8 3.3 %collective-permute-start.8 = (f32[64,128]{1,0:T(8,128)S(1)}, f32[64,128]{1,0:T(8,128)S(1)}, u32[]{:S(2)}, u32[]{:S(2)}) collective-permute-start(f32[64,128]{1,0:T(8,128)S(1)} %fusion.27), channel_id=1, source_target_pairs={{0,24},{8,0},{16,8},{24,16},{1,25},{9,1},{17,9},{25,17},{2,26},{10... | collective-permute-start | bytes 98312 | tf_op jit(solution)/shard_map/ppermute | solution.py:37
  203.2 3.3 %collective-permute-start.7 = (f32[64,128]{1,0:T(8,128)S(1)}, f32[64,128]{1,0:T(8,128)S(1)}, u32[]{:S(2)}, u32[]{:S(2)}) collective-permute-start(f32[64,128]{1,0:T(8,128)S(1)} %collective-permute-done.6), channel_id=1, source_target_pairs={{0,8},{8,16},{16,24},{24,0},{1,9},{9,17},{17,25},{25,1},{2,10},{10... | collective-permute-start | bytes 98312 | tf_op jit(solution)/shard_map/ppermute | solution.py:35
  210.4 3.4 %collective-permute-start.9 = (f32[64,128]{1,0:T(8,128)S(1)}, f32[64,128]{1,0:T(8,128)S(1)}, u32[]{:S(2)}, u32[]{:S(2)}) collective-permute-start(f32[64,128]{1,0:T(8,128)S(1)} %fusion.29), channel_id=1, source_target_pairs={{0,8},{8,16},{16,24},{24,0},{1,9},{9,17},{17,25},{25,1},{2,10},{10... | collective-permute-start | bytes 98312 | tf_op jit(solution)/shard_map/ppermute | solution.py:35
  210.5 3.3 %collective-permute-start.11 = (f32[64,128]{1,0:T(8,128)S(1)}, f32[64,128]{1,0:T(8,128)S(1)}, u32[]{:S(2)}, u32[]{:S(2)}) collective-permute-start(f32[64,128]{1,0:T(8,128)S(1)} %fusion.29), channel_id=1, source_target_pairs={{0,24},{8,0},{16,8},{24,16},{1,25},{9,1},{17,9},{25,17},{2,26},{10... | collective-permute-start | bytes 98312 | tf_op jit(solution)/shard_map/ppermute | solution.py:37
  213.8 3.3 %collective-permute-start.10 = (f32[64,128]{1,0:T(8,128)S(1)}, f32[64,128]{1,0:T(8,128)S(1)}, u32[]{:S(2)}, u32[]{:S(2)}) collective-permute-start(f32[64,128]{1,0:T(8,128)S(1)} %collective-permute-done.9), channel_id=1, source_target_pairs={{0,8},{8,16},{16,24},{24,0},{1,9},{9,17},{17,25},{25,1},{2,10},{10... | collective-permute-start | bytes 98312 | tf_op jit(solution)/shard_map/ppermute | solution.py:35
  218.8 32.2 %copy-start.2 = (f32[64,128]{1,0:T(8,128)S(1)}, f32[64,128]{1,0:T(8,128)}, u32[]{:S(2)}) copy-start(f32[64,128]{1,0:T(8,128)} %get-tuple-element.13) | copy-start | bytes 98308
  221.1 3.4 %collective-permute-start.12 = (f32[64,128]{1,0:T(8,128)S(1)}, f32[64,128]{1,0:T(8,128)S(1)}, u32[]{:S(2)}, u32[]{:S(2)}) collective-permute-start(f32[64,128]{1,0:T(8,128)S(1)} %fusion.31), channel_id=1, source_target_pairs={{0,8},{8,16},{16,24},{24,0},{1,9},{9,17},{17,25},{25,1},{2,10},{10... | collective-permute-start | bytes 98312 | tf_op jit(solution)/shard_map/ppermute | solution.py:35
  221.2 3.4 %collective-permute-start.14 = (f32[64,128]{1,0:T(8,128)S(1)}, f32[64,128]{1,0:T(8,128)S(1)}, u32[]{:S(2)}, u32[]{:S(2)}) collective-permute-start(f32[64,128]{1,0:T(8,128)S(1)} %fusion.31), channel_id=1, source_target_pairs={{0,24},{8,0},{16,8},{24,16},{1,25},{9,1},{17,9},{25,17},{2,26},{10... | collective-permute-start | bytes 98312 | tf_op jit(solution)/shard_map/ppermute | solution.py:37
  224.5 3.3 %collective-permute-start.13 = (f32[64,128]{1,0:T(8,128)S(1)}, f32[64,128]{1,0:T(8,128)S(1)}, u32[]{:S(2)}, u32[]{:S(2)}) collective-permute-start(f32[64,128]{1,0:T(8,128)S(1)} %collective-permute-done.12), channel_id=1, source_target_pairs={{0,8},{8,16},{16,24},{24,0},{1,9},{9,17},{17,25},{25,1},{2,10},{10... | collective-permute-start | bytes 98312 | tf_op jit(solution)/shard_map/ppermute | solution.py:35
  231.7 3.4 %collective-permute-start.15 = (f32[64,128]{1,0:T(8,128)S(1)}, f32[64,128]{1,0:T(8,128)S(1)}, u32[]{:S(2)}, u32[]{:S(2)}) collective-permute-start(f32[64,128]{1,0:T(8,128)S(1)} %fusion.33), channel_id=1, source_target_pairs={{0,8},{8,16},{16,24},{24,0},{1,9},{9,17},{17,25},{25,1},{2,10},{10... | collective-permute-start | bytes 98312 | tf_op jit(solution)/shard_map/ppermute | solution.py:35
  231.9 3.5 %collective-permute-start.17 = (f32[64,128]{1,0:T(8,128)S(1)}, f32[64,128]{1,0:T(8,128)S(1)}, u32[]{:S(2)}, u32[]{:S(2)}) collective-permute-start(f32[64,128]{1,0:T(8,128)S(1)} %fusion.33), channel_id=1, source_target_pairs={{0,24},{8,0},{16,8},{24,16},{1,25},{9,1},{17,9},{25,17},{2,26},{10... | collective-permute-start | bytes 98312 | tf_op jit(solution)/shard_map/ppermute | solution.py:37
  235.1 3.5 %collective-permute-start.16 = (f32[64,128]{1,0:T(8,128)S(1)}, f32[64,128]{1,0:T(8,128)S(1)}, u32[]{:S(2)}, u32[]{:S(2)}) collective-permute-start(f32[64,128]{1,0:T(8,128)S(1)} %collective-permute-done.15), channel_id=1, source_target_pairs={{0,8},{8,16},{16,24},{24,0},{1,9},{9,17},{17,25},{25,1},{2,10},{10... | collective-permute-start | bytes 98312 | tf_op jit(solution)/shard_map/ppermute | solution.py:35
  242.6 3.4 %collective-permute-start.18 = (f32[64,128]{1,0:T(8,128)S(1)}, f32[64,128]{1,0:T(8,128)S(1)}, u32[]{:S(2)}, u32[]{:S(2)}) collective-permute-start(f32[64,128]{1,0:T(8,128)S(1)} %fusion.35), channel_id=1, source_target_pairs={{0,8},{8,16},{16,24},{24,0},{1,9},{9,17},{17,25},{25,1},{2,10},{10... | collective-permute-start | bytes 98312 | tf_op jit(solution)/shard_map/ppermute | solution.py:35
  242.7 3.4 %collective-permute-start.20 = (f32[64,128]{1,0:T(8,128)S(1)}, f32[64,128]{1,0:T(8,128)S(1)}, u32[]{:S(2)}, u32[]{:S(2)}) collective-permute-start(f32[64,128]{1,0:T(8,128)S(1)} %fusion.35), channel_id=1, source_target_pairs={{0,24},{8,0},{16,8},{24,16},{1,25},{9,1},{17,9},{25,17},{2,26},{10... | collective-permute-start | bytes 98312 | tf_op jit(solution)/shard_map/ppermute | solution.py:37
  246.0 3.3 %collective-permute-start.19 = (f32[64,128]{1,0:T(8,128)S(1)}, f32[64,128]{1,0:T(8,128)S(1)}, u32[]{:S(2)}, u32[]{:S(2)}) collective-permute-start(f32[64,128]{1,0:T(8,128)S(1)} %collective-permute-done.18), channel_id=1, source_target_pairs={{0,8},{8,16},{16,24},{24,0},{1,9},{9,17},{17,25},{25,1},{2,10},{10... | collective-permute-start | bytes 98312 | tf_op jit(solution)/shard_map/ppermute | solution.py:35
  253.2 3.4 %collective-permute-start.21 = (f32[64,128]{1,0:T(8,128)S(1)}, f32[64,128]{1,0:T(8,128)S(1)}, u32[]{:S(2)}, u32[]{:S(2)}) collective-permute-start(f32[64,128]{1,0:T(8,128)S(1)} %fusion.37), channel_id=1, source_target_pairs={{0,8},{8,16},{16,24},{24,0},{1,9},{9,17},{17,25},{25,1},{2,10},{10... | collective-permute-start | bytes 98312 | tf_op jit(solution)/shard_map/ppermute | solution.py:35
  253.4 3.4 %collective-permute-start.23 = (f32[64,128]{1,0:T(8,128)S(1)}, f32[64,128]{1,0:T(8,128)S(1)}, u32[]{:S(2)}, u32[]{:S(2)}) collective-permute-start(f32[64,128]{1,0:T(8,128)S(1)} %fusion.37), channel_id=1, source_target_pairs={{0,24},{8,0},{16,8},{24,16},{1,25},{9,1},{17,9},{25,17},{2,26},{10... | collective-permute-start | bytes 98312 | tf_op jit(solution)/shard_map/ppermute | solution.py:37
  256.6 3.3 %collective-permute-start.22 = (f32[64,128]{1,0:T(8,128)S(1)}, f32[64,128]{1,0:T(8,128)S(1)}, u32[]{:S(2)}, u32[]{:S(2)}) collective-permute-start(f32[64,128]{1,0:T(8,128)S(1)} %collective-permute-done.21), channel_id=1, source_target_pairs={{0,8},{8,16},{16,24},{24,0},{1,9},{9,17},{17,25},{25,1},{2,10},{10... | collective-permute-start | bytes 98312 | tf_op jit(solution)/shard_map/ppermute | solution.py:35
Sparse Core Ops, SparseCore 0:
  9.4 77.7 all-gather.2
  91.4 70.6 all-reduce.3
  163.8 21.9 all-gather.4
